TPU v7x, 128 devices: a whole 4x4x4 slice. The times are simulated.
128 devices in a mesh: bin: 4 (over y_lo, core), tile: 32 (over z, x, y_hi).
Axes of the slice: x: 4, y: 4 (y_hi: 2, y_lo: 2; y = y_hi * 2 + y_lo), z: 4, core: 2. Of those that a mesh axis runs over, the one named last changes fastest.
Arguments:
- shear_one: float32 [4, 4096, 4096], P('bin', 'tile'), may hold values from -6 to 6
- shear_two: float32 [4, 4096, 4096], P('bin', 'tile'), may hold values from -6 to 6
- weights: float32 [4, 4], replicated, may hold values from 0.2 to 1
Outputs:
- convergence: float32 [4, 4096, 4096], P('bin', 'tile')
All inputs are finite; a program needn't handle non-finite values.
Results may differ from a plain program's by a relative error of at most 0.000071.
Values sent between devices are 32-bit elements; how exact they have to be, the bound alone decides.
A program may use at most 128 MiB of HBM per device.

v0:
```python
import functools

import jax
import jax.numpy as jnp
import ml_dtypes
import numpy as np
from jax import lax
from jax.experimental import pallas as pl
from jax.experimental.pallas import tpu as pltpu
from jax.sharding import PartitionSpec as P

N = 4096
A = 32
L = 128
DEV = 128
BINS = 4
F32 = jnp.float32
BF16 = jnp.bfloat16


def hi_lo(matrix):
    hi = matrix.astype(ml_dtypes.bfloat16)
    lo = (matrix - hi.astype(np.float64)).astype(ml_dtypes.bfloat16)
    return np.stack([hi, lo])


def tables():
    lane = np.arange(L)
    angle = 2.0 * np.pi * ((lane[:, None] * lane[None, :]) % L) / L
    c, s = np.cos(angle), np.sin(angle)
    fwd = np.block([[c, s], [-s, c]])
    slot = np.arange(64)
    a0 = 2.0 * np.pi * ((slot[:, None] * lane[None, :]) % L) / L
    a16 = 2.0 * np.pi * (((16 + 32 * slot[:, None]) * lane[None, :]) % N) / N
    first = np.zeros((256, 256))
    first[0:64, 0:128] = np.cos(a0)
    first[128:192, 0:128] = -np.sin(a0)
    first[128, 0:128] = (-1.0) ** lane
    first[64:128, 128:256] = np.cos(a16)
    first[192:256, 128:256] = -np.sin(a16)
    last = 2.0 * first.copy()
    last[0, 0:128] = 1.0
    last[128, 0:128] = (-1.0) ** lane
    k = np.arange(A)
    tw = 2.0 * np.pi * ((k[:, None] * lane[None, :]) % N) / N
    twid = np.stack([np.cos(tw), np.sin(tw)], 1).astype(np.float32)
    twid = np.broadcast_to(twid[:, :, None, :], (A, 2, 8, L)).copy()
    return dict(
        row=np.stack([hi_lo(first), hi_lo(fwd)]),
        colf=hi_lo(fwd.T),
        coli=hi_lo(fwd),
        back=np.stack([hi_lo(last), hi_lo(fwd)]),
        twid=twid,
    )


def fft(xs, sign):
    n = len(xs)
    if n == 1:
        return xs
    even, odd = fft(xs[0::2], sign), fft(xs[1::2], sign)
    out = [None] * n
    h = n // 2
    root = np.float32(np.sqrt(0.5))
    for k in range(h):
        er, ei = even[k]
        r, i = odd[k]
        if k == 0:
            tr, ti = r, i
        elif 4 * k == n:
            tr, ti = (-i, r) if sign > 0 else (i, -r)
            if sign > 0:
                out[k], out[k + h] = (er - i, ei + r), (er + i, ei - r)
            else:
                out[k], out[k + h] = (er + i, ei - r), (er - i, ei + r)
            continue
        elif 8 * k == n:
            tr, ti = ((r - i) * root, (r + i) * root) if sign > 0 else ((r + i) * root, (i - r) * root)
        elif 8 * k == 3 * n:
            if sign > 0:
                pr, pi = (r + i) * root, (r - i) * root
                out[k], out[k + h] = (er - pr, ei + pi), (er + pr, ei - pi)
            else:
                pr, pi = (i - r) * root, (r + i) * root
                out[k], out[k + h] = (er + pr, ei - pi), (er - pr, ei + pi)
            continue
        else:
            c = np.float32(np.cos(2 * np.pi * k / n))
            s = np.float32(sign * np.sin(2 * np.pi * k / n))
            tr, ti = r * c - i * s, r * s + i * c
        out[k], out[k + h] = (er + tr, ei + ti), (er - tr, ei - ti)
    return out


def rfft(xs):
    n = len(xs)
    if n == 2:
        return [(xs[0] + xs[1], None), (xs[0] - xs[1], None)]
    even, odd = rfft(xs[0::2]), rfft(xs[1::2])
    out = [None] * (n // 2 + 1)
    for k in range(n // 4 + 1):
        if k == 0:
            out[0] = (even[0][0] + odd[0][0], None)
            out[n // 2] = (even[0][0] - odd[0][0], None)
        elif 4 * k == n:
            out[k] = (even[k][0], -odd[k][0])
        else:
            er, ei = even[k]
            r, i = odd[k]
            if 8 * k == n:
                root = np.float32(np.sqrt(0.5))
                tr, ti = (r + i) * root, (i - r) * root
            else:
                c = np.float32(np.cos(2 * np.pi * k / n))
                s = np.float32(np.sin(2 * np.pi * k / n))
                tr, ti = r * c + i * s, i * c - r * s
            out[k] = (er + tr, ei + ti)
            out[n // 2 - k] = (er - tr, ti - ei)
    return out


def irfft(X, n):
    if n == 2:
        a, b = X[0][0], X[1][0]
        return [a + b, a - b]
    h = n // 2
    even, odd = [None] * (h // 2 + 1), [None] * (h // 2 + 1)
    for k in range(h // 2 + 1):
        if k == 0:
            even[0] = (X[0][0] + X[h][0], None)
            odd[0] = (X[0][0] - X[h][0], None)
        elif 2 * k == h:
            even[k] = (X[k][0] + X[k][0], None)
            odd[k] = (-(X[k][1] + X[k][1]), None)
        else:
            ar, ai = X[k]
            br, bi = X[h - k]
            even[k] = (ar + br, ai - bi)
            dr, di = ar - br, ai + bi
            if 4 * k == h:
                root = np.float32(np.sqrt(0.5))
                odd[k] = ((dr - di) * root, (dr + di) * root)
            else:
                c = np.float32(np.cos(2 * np.pi * k / n))
                s = np.float32(np.sin(2 * np.pi * k / n))
                odd[k] = (dr * c - di * s, dr * s + di * c)
    e, o = irfft(even, h), irfft(odd, h)
    out = [None] * n
    out[0::2] = e
    out[1::2] = o
    return out


def split(x):
    hi = x.astype(BF16)
    lo = (x - hi.astype(F32)).astype(BF16)
    return hi, lo


ROWS = 16
STEPS = 128 // ROWS


def row_kernel(g1_ref, g2_ref, tw_ref, w_ref, *refs):
    outs, y_ref = refs[:-1], refs[-1]
    i = pl.program_id(0)

    @pl.when(i < STEPS)
    def _():
        for comp, g_ref in enumerate((g1_ref, g2_ref)):
            for j in range(ROWS // 8):
                xs = [g_ref[8 * j : 8 * j + 8, L * p : L * p + L] for p in range(A)]
                X = rfft(xs)
                rows = pl.ds(pl.multiple_of(128 * comp + i * ROWS + 8 * j, 8), 8)
                y_ref[0, rows, 0:L] = X[0][0]
                y_ref[0, rows, L : 2 * L] = X[16][0]
                for k in range(1, 16):
                    r, m = X[k]
                    c, s = tw_ref[k, 0], tw_ref[k, 1]
                    y_ref[k, rows, 0:L] = r * c + m * s
                    y_ref[k, rows, L : 2 * L] = m * c - r * s

    @pl.when(i >= STEPS)
    def _():
        k = i - STEPS
        hi, lo = split(y_ref[k])
        sel = jnp.minimum(k, 1)
        whi, wlo = w_ref[sel, 0], w_ref[sel, 1]
        dims = (((1,), (1,)), ((), ()))
        dot = functools.partial(lax.dot_general, dimension_numbers=dims, preferred_element_type=F32)
        out = dot(whi, hi) + (dot(whi, lo) + dot(wlo, hi))
        for h in range(2):
            for c in range(2):
                for d in range(8):
                    at = 128 * c + 64 * h + 8 * d
                    outs[h][d, c] = out[at : at + 8]


def row_stage(g1, g2, tab):
    g1, g2 = g1.reshape(128, N), g2.reshape(128, N)
    last = STEPS - 1
    return pl.pallas_call(
        row_kernel,
        grid=(STEPS + 16,),
        in_specs=[
            pl.BlockSpec((ROWS, N), lambda i: (jnp.minimum(i, last), 0)),
            pl.BlockSpec((ROWS, N), lambda i: (jnp.minimum(i, last), 0)),
            pl.BlockSpec((A, 2, 8, L), lambda i: (0, 0, 0, 0)),
            pl.BlockSpec((2, 2, 256, 256), lambda i: (0, 0, 0, 0)),
        ],
        out_specs=[pl.BlockSpec((8, 2, 8, 256), lambda i: (jnp.maximum(i - STEPS, 0), 0, 0, 0))] * 2,
        out_shape=[jax.ShapeDtypeStruct((DEV, 2, 8, 256), F32)] * 2,
        scratch_shapes=[pltpu.VMEM((16, 256, 256), F32)],
        cost_estimate=pl.CostEstimate(flops=10**9, bytes_accessed=8 * 2**20, transcendentals=0),
        name="rows",
    )(g1, g2, tab["twid"], tab["row"])


GROUP = 4


def col_kernel(half, wgt_ref, x_ref, tw_ref, wf_ref, wi_ref, out_ref, y_ref, z_ref):
    i = pl.program_id(0)
    dev = lax.axis_index(("bin", "tile"))
    group, part = dev // 8, dev % 8
    sub = lax.broadcasted_iota(jnp.int32, (8, L), 0)
    lane = lax.broadcasted_iota(jnp.int32, (8, L), 1)
    if half == 0:
        packed = jnp.logical_and(sub == 0, dev == 0)

    @pl.when(i < BINS)
    def _():
        if half == 0:
            sign = jnp.where(lane % 2 == 0, 1.0, -1.0).astype(F32)
            total = x_ref[0, 1, :, L : 2 * L]
            for t in range(1, A):
                total = total + x_ref[t, 1, :, L : 2 * L]
            corner = sign * (jnp.sum(total * sign, axis=1, keepdims=True) * np.float32(-1.0 / N))
        for R in range(2):
            xs = []
            for t in range(A):
                re = x_ref[t, 0, :, R * L : R * L + L]
                im = x_ref[t, 1, :, R * L : R * L + L]
                if half == 0:
                    if R == 0:
                        im = jnp.where(packed, corner, im)
                    else:
                        re = jnp.where(packed, 0.0, re)
                        im = jnp.where(packed, x_ref[t, 1, :, 0:L], im)
                xs.append((re, im))
            X = fft(xs, -1)
            rows = pl.ds(pl.multiple_of(32 * R + 8 * i, 8), 8)
            for k in range(A):
                r, m = X[k]
                if k:
                    c, s = tw_ref[k, 0], tw_ref[k, 1]
                    r, m = r * c + m * s, m * c - r * s
                y_ref[k, rows, 0:L] = r
                y_ref[k, rows, L : 2 * L] = m

    @pl.when(jnp.logical_and(i >= BINS, i < BINS + A // GROUP))
    def _():
        base = (i - BINS) * GROUP
        hi, lo = split(y_ref[pl.ds(base, GROUP)].reshape(GROUP * 64, 256))
        dot = functools.partial(jnp.dot, preferred_element_type=F32)
        G = dot(hi, wf_ref[0]) + (dot(lo, wf_ref[0]) + dot(hi, wf_ref[1]))
        at = 8 * part + sub
        col = jnp.where(group == 0, 32 * at + 16 * half, group + 32 * (64 * half + at))
        col = jnp.where(col < N // 2, col, col - N).astype(F32)
        scale = np.float32(1.0 / (N * N))
        w = [[wgt_ref[j, b] * scale for b in range(j + 1)] for j in range(BINS)]
        rows = []
        for kk in range(GROUP):
            u = base + kk + A * lane
            nyquist = u == N // 2
            row = jnp.where(u < N // 2, u, u - N).astype(F32)
            row2 = row * row

            def kern(l1):
                q = jnp.maximum(l1 * l1 + row2, 1.0)
                return (l1 * l1 - row2) / q, (2.0 * l1) * row / q

            a, b = kern(col)
            ar, ai = a, jnp.where(nyquist, -b, 0.0)
            br = jnp.where(nyquist, 0.0, b)
            if half == 0:
                a2, b2 = kern(jnp.full_like(col, -N // 2))
                br = jnp.where(packed, a2, br)
                bi = jnp.where(jnp.logical_and(packed, jnp.logical_not(nyquist)), -b2, 0.0)
            H = []
            for b_ in range(BINS):
                o1, o2 = kk * 64 + 8 * b_, kk * 64 + 32 + 8 * b_
                g1r, g1i = G[o1 : o1 + 8, 0:L], G[o1 : o1 + 8, L : 2 * L]
                g2r, g2i = G[o2 : o2 + 8, 0:L], G[o2 : o2 + 8, L : 2 * L]
                hr = ar * g1r - ai * g1i + br * g2r
                hm = ar * g1i + ai * g1r + br * g2i
                if half == 0:
                    hr, hm = hr - bi * g2i, hm + bi * g2r
                H.append((hr, hm))
            for j in range(BINS):
                fr, fi = H[0][0] * w[j][0], H[0][1] * w[j][0]
                for b_ in range(1, j + 1):
                    fr, fi = fr + H[b_][0] * w[j][b_], fi + H[b_][1] * w[j][b_]
                rows.append(jnp.concatenate([fr, fi], axis=1))
        hi, lo = split(jnp.concatenate(rows, axis=0))
        Z = dot(hi, wi_ref[0]) + (dot(lo, wi_ref[0]) + dot(hi, wi_ref[1]))
        for kk in range(GROUP):
            c, s = tw_ref[base + kk, 0], tw_ref[base + kk, 1]
            for j in range(BINS):
                o = 32 * kk + 8 * j
                r, m = Z[o : o + 8, 0:L], Z[o : o + 8, L : 2 * L]
                z_ref[base + kk, 8 * j : 8 * j + 8, 0:L] = r * c - m * s
                z_ref[base + kk, 8 * j : 8 * j + 8, L : 2 * L] = m * c + r * s

    @pl.when(i >= BINS + A // GROUP)
    def _():
        j = i - (BINS + A // GROUP)
        rows = pl.ds(pl.multiple_of(8 * j, 8), 8)
        xs = [(z_ref[k, rows, 0:L], z_ref[k, rows, L : 2 * L]) for k in range(A)]
        for t, (r, m) in enumerate(fft(xs, 1)):
            out_ref[t, 0] = r
            out_ref[t, 1] = m


def col_stage(x, weights, tab, half):
    before = BINS + A // GROUP
    return pl.pallas_call(
        functools.partial(col_kernel, half),
        grid=(before + BINS,),
        in_specs=[
            pl.BlockSpec(memory_space=pltpu.SMEM),
            pl.BlockSpec((A, 2, 8, 256), lambda i: (jnp.minimum(i, BINS - 1), 0, 0, 0)),
            pl.BlockSpec((A, 2, 8, L), lambda i: (0, 0, 0, 0)),
            pl.BlockSpec((2, 256, 256), lambda i: (0, 0, 0)),
            pl.BlockSpec((2, 256, 256), lambda i: (0, 0, 0)),
        ],
        out_specs=pl.BlockSpec((A, 2, 8, L), lambda i: (jnp.maximum(i - before, 0), 0, 0, 0)),
        out_shape=jax.ShapeDtypeStruct((DEV, 2, 8, L), F32),
        scratch_shapes=[pltpu.VMEM((A, 64, 256), F32), pltpu.VMEM((A, 32, 256), F32)],
        cost_estimate=pl.CostEstimate(flops=10**9, bytes_accessed=4 * 2**20, transcendentals=0),
        name="cols%d" % half,
    )(weights, x, tab["twid"], tab["colf"], tab["coli"])


def back_kernel(x0_ref, x1_ref, tw_ref, w_ref, out_ref, z_ref):
    i = pl.program_id(0)

    @pl.when(i < 16)
    def _():
        parts = []
        for c in range(2):
            for ref in (x0_ref, x1_ref):
                for d in range(8):
                    parts.append(ref[d, c])
        hi, lo = split(jnp.concatenate(parts, axis=0).T)
        sel = jnp.minimum(i, 1)
        dot = functools.partial(jnp.dot, preferred_element_type=F32)
        Z = dot(hi, w_ref[sel, 0]) + (dot(lo, w_ref[sel, 0]) + dot(hi, w_ref[sel, 1]))
        c, s = tw_ref[i, 0, 0:1], tw_ref[i, 1, 0:1]
        r, m = Z[:, 0:L], Z[:, L : 2 * L]
        z_ref[i, :, 0:L] = r * c - m * s
        z_ref[i, :, L : 2 * L] = m * c + r * s

    @pl.when(i >= 16)
    def _():
        for j in range(ROWS // 8):
            rows = pl.ds(pl.multiple_of((i - 16) * ROWS + 8 * j, 8), 8)
            X = [(z_ref[0, rows, 0:L], None)]
            X += [(z_ref[k, rows, 0:L], z_ref[k, rows, L : 2 * L]) for k in range(1, 16)]
            X += [(z_ref[0, rows, L : 2 * L], None)]
            for p, v in enumerate(irfft(X, A)):
                out_ref[8 * j : 8 * j + 8, L * p : L * p + L] = v


def back_stage(x0, x1, tab):
    return pl.pallas_call(
        back_kernel,
        grid=(16 + STEPS,),
        in_specs=[
            pl.BlockSpec((8, 2, 8, L), lambda i: (jnp.minimum(i, 15), 0, 0, 0)),
            pl.BlockSpec((8, 2, 8, L), lambda i: (jnp.minimum(i, 15), 0, 0, 0)),
            pl.BlockSpec((A, 2, 8, L), lambda i: (0, 0, 0, 0)),
            pl.BlockSpec((2, 2, 256, 256), lambda i: (0, 0, 0, 0)),
        ],
        out_specs=pl.BlockSpec((ROWS, N), lambda i: (jnp.maximum(i - 16, 0), 0)),
        out_shape=jax.ShapeDtypeStruct((128, N), F32),
        scratch_shapes=[pltpu.VMEM((16, 128, 256), F32)],
        cost_estimate=pl.CostEstimate(flops=10**9, bytes_accessed=4 * 2**20, transcendentals=0),
        name="back",
    )(x0, x1, tab["twid"], tab["back"])


def exchange(x):
    return lax.all_to_all(x, ("bin", "tile"), split_axis=0, concat_axis=0, tiled=True)


def on_device(shear_one, shear_two, weights):
    tab = {k: jnp.asarray(v) for k, v in tables().items()}
    halves = row_stage(shear_one, shear_two, tab)
    back = []
    for half in range(2):
        got = exchange(halves[half])
        back.append(exchange(col_stage(got, weights, tab, half)))
    return back_stage(back[0], back[1], tab).reshape(1, 128, N)


def solution(mesh):
    spec = P("bin", "tile", None)
    return jax.shard_map(
        on_device, mesh=mesh, in_specs=(spec, spec, P()), out_specs=spec, check_vma=False
    )
```

profile of v0, /device:TPU:1, one launch (start us, length us, event | category | flops | bytes accessed | tf_op | source)
XLA Modules:
  0.0 151.9 jit_solution(15435158946264907474)
XLA Ops:
  0.0 14.0 %rows.1 = (f32[128,2,8,256]{3,2,1,0:T(8,128)}, f32[128,2,8,256]{3,2,1,0:T(8,128)}) custom-call(f32[128,4096]{1,0:T(8,128)} %bitcast.3, f32[128,4096]{1,0:T(8,128)} %bitcast.4, f32[32,2,8,128]{3,2,1,0:T(8,128)} %constant.14.clone.tw_ref, bf16[2,2,256,256]{3,2,1,0:T(8,128)(2,1)} %constant.10.clone.w_ref), custom_call_target="tpu_custom_call" | custom-call | flops 1000000000 | bytes 8388608 | tf_op jit(solution)/shard_map/rows/pallas_call | solution.py:202
  14.0 42.0 %all_to_all.20.x_ref = f32[128,2,8,256]{3,2,1,0:T(8,128)} all-to-all(f32[128,2,8,256]{3,2,1,0:T(8,128)} %get-tuple-element.7), channel_id=1, replica_groups=mesh['bin'=4,'tile'=32] {'bin','tile'}, dimensions={0} | all-to-all | bytes 4194304 | tf_op jit(solution)/shard_map/all_to_all | solution.py:394
  56.0 4.4 %all-to-all-start.2 = ((f32[128,2,8,256]{3,2,1,0:T(8,128)}), f32[128,2,8,256]{3,2,1,0:T(8,128)S(1)}, u32[]{:S(2)}, u32[]{:S(2)}) async-start(f32[128,2,8,256]{3,2,1,0:T(8,128)} %get-tuple-element.8), calls=%async_computation.2 | async-start | bytes 4194304 | tf_op jit(solution)/shard_map/all_to_all | solution.py:394
  60.4 10.2 %cols0.1 = f32[128,2,8,128]{3,2,1,0:T(8,128)} custom-call(f32[4,4]{1,0:T(4,128)} %wgt_ref.3, f32[128,2,8,256]{3,2,1,0:T(8,128)} %all_to_all.20.x_ref, f32[32,2,8,128]{3,2,1,0:T(8,128)} %constant.14.clone.tw_ref, bf16[2,256,256]{2,1,0:T(8,128)(2,1)} %constant.11.clone.wf_ref, bf16[2,256,256]{2,1,0:T(8,128)(2,1)} %constant.12.clone.wi_ref), custom_call_target="tpu_custom_call" | custom-call | flops 1000000000 | bytes 4194304 | tf_op jit(solution)/shard_map/cols0/pallas_call | solution.py:327
  70.6 20.2 %all-to-all-done.2.x_ref = f32[128,2,8,256]{3,2,1,0:T(8,128)S(1)} async-done(((f32[128,2,8,256]{3,2,1,0:T(8,128)}), f32[128,2,8,256]{3,2,1,0:T(8,128)S(1)}, u32[]{:S(2)}, u32[]{:S(2)}) %all-to-all-start.2) | async-done | bytes 2097184 | tf_op jit(solution)/shard_map/all_to_all | solution.py:394
  90.8 0.0 copy-start
  90.8 4.4 %all-to-all-start.1 = ((f32[128,2,8,128]{3,2,1,0:T(8,128)}), f32[128,2,8,128]{3,2,1,0:T(8,128)S(1)}, u32[]{:S(2)}, u32[]{:S(2)}) async-start(f32[128,2,8,128]{3,2,1,0:T(8,128)} %cols0.1), calls=%async_computation.1 | async-start | bytes 2097152 | tf_op jit(solution)/shard_map/all_to_all | solution.py:394
  95.2 0.0 copy-done
  95.2 9.8 %cols1.1 = f32[128,2,8,128]{3,2,1,0:T(8,128)} custom-call(f32[4,4]{1,0:T(4,128)} %wgt_ref.3, f32[128,2,8,256]{3,2,1,0:T(8,128)} %copy-done, f32[32,2,8,128]{3,2,1,0:T(8,128)} %constant.14.clone.tw_ref, bf16[2,256,256]{2,1,0:T(8,128)(2,1)} %constant.11.clone.wf_ref, bf16[2,256,256]{2,1,0:T(8,128)(2,1)} %constant.12.clone.wi_ref), custom_call_target="tpu_custom_call" | custom-call | flops 1000000000 | bytes 4194304 | tf_op jit(solution)/shard_map/cols1/pallas_call | solution.py:327
  105.0 9.6 %all-to-all-done.1.x0_ref = f32[128,2,8,128]{3,2,1,0:T(8,128)S(1)} async-done(((f32[128,2,8,128]{3,2,1,0:T(8,128)}), f32[128,2,8,128]{3,2,1,0:T(8,128)S(1)}, u32[]{:S(2)}, u32[]{:S(2)}) %all-to-all-start.1) | async-done | bytes 1048608 | tf_op jit(solution)/shard_map/all_to_all | solution.py:394
  114.6 0.0 copy-start.1
  114.6 24.0 %all_to_all.21.x1_ref = f32[128,2,8,128]{3,2,1,0:T(8,128)} all-to-all(f32[128,2,8,128]{3,2,1,0:T(8,128)} %cols1.1), channel_id=1, replica_groups=mesh['bin'=4,'tile'=32] {'bin','tile'}, dimensions={0} | all-to-all | bytes 2097152 | tf_op jit(solution)/shard_map/all_to_all | solution.py:394
  138.6 0.0 copy-done.1
  138.6 13.3 %back.1 = f32[128,4096]{1,0:T(8,128)} custom-call(f32[128,2,8,128]{3,2,1,0:T(8,128)} %copy-done.1, f32[128,2,8,128]{3,2,1,0:T(8,128)} %all_to_all.21.x1_ref, f32[32,2,8,128]{3,2,1,0:T(8,128)} %constant.14.clone.tw_ref, bf16[2,2,256,256]{3,2,1,0:T(8,128)(2,1)} %constant.13.clone.w_ref), custom_call_target="tpu_custom_call" | custom-call | flops 1000000000 | bytes 4194304 | tf_op jit(solution)/shard_map/back/pallas_call | solution.py:376
Async XLA Ops:
  56.0 34.8 %all-to-all-start.2 = ((f32[128,2,8,256]{3,2,1,0:T(8,128)}), f32[128,2,8,256]{3,2,1,0:T(8,128)S(1)}, u32[]{:S(2)}, u32[]{:S(2)}) async-start(f32[128,2,8,256]{3,2,1,0:T(8,128)} %get-tuple-element.8), calls=%async_computation.2 | async-start | bytes 4194304 | tf_op jit(solution)/shard_map/all_to_all | solution.py:394
  90.8 4.4 %copy-start = (f32[128,2,8,256]{3,2,1,0:T(8,128)}, f32[128,2,8,256]{3,2,1,0:T(8,128)S(1)}, u32[]{:S(2)}) copy-start(f32[128,2,8,256]{3,2,1,0:T(8,128)S(1)} %all-to-all-done.2.x_ref) | copy-start | bytes 6291460
  90.8 23.8 %all-to-all-start.1 = ((f32[128,2,8,128]{3,2,1,0:T(8,128)}), f32[128,2,8,128]{3,2,1,0:T(8,128)S(1)}, u32[]{:S(2)}, u32[]{:S(2)}) async-start(f32[128,2,8,128]{3,2,1,0:T(8,128)} %cols0.1), calls=%async_computation.1 | async-start | bytes 2097152 | tf_op jit(solution)/shard_map/all_to_all | solution.py:394
  114.6 24.0 %copy-start.1 = (f32[128,2,8,128]{3,2,1,0:T(8,128)}, f32[128,2,8,128]{3,2,1,0:T(8,128)S(1)}, u32[]{:S(2)}) copy-start(f32[128,2,8,128]{3,2,1,0:T(8,128)S(1)} %all-to-all-done.1.x0_ref) | copy-start | bytes 3145732
where the time goes:
time: 153 us; the launch traced here: 152 us
  blocking collectives  66 us (43%)
  Pallas kernels  47.2 us (31%)
  waiting for transfers between devices  29.8 us (19%)
  starting transfers between devices  8.84 us (6%)
    all_to_all x2, blocking collectives, exchange(): lax.all_to_all(x, ('bin', 'tile'), split_axis=0, concat_axis=0, tiled=True)  66 us
    all_to_all x2, waiting for transfers between devices, exchange(): lax.all_to_all(x, ('bin', 'tile'), split_axis=0, concat_axis=0, tiled=True)  29.8 us
    pallas_call x2, Pallas kernels, col_stage(): pl.pallas_call(functools.partial(col_kernel, half), grid=(before + BINS,)...  20 us
    pallas_call x1, Pallas kernels, row_stage(): pl.pallas_call(row_kernel, grid=(STEPS + 16,), in_specs=[pl.BlockSpec((RO...  14 us
    pallas_call x1, Pallas kernels, back_stage(): pl.pallas_call(back_kernel, grid=(16 + STEPS,), in_specs=[pl.BlockSpec((8...  13.3 us
    all_to_all x2, starting transfers between devices, exchange(): lax.all_to_all(x, ('bin', 'tile'), split_axis=0, concat_axis=0, tiled=True)  8.84 us
  transfers between devices with their start and end apart: 2, of which 2 were waited for; matrix products, arithmetic and copies ran while one was open for 0% of the time, Pallas kernels for 13%

commit v1 on v0

v1 whole, which is shorter than its diff:
```python
import functools

import jax
import jax.numpy as jnp
import ml_dtypes
import numpy as np
from jax import lax
from jax.experimental import pallas as pl
from jax.experimental.pallas import tpu as pltpu
from jax.sharding import PartitionSpec as P

N = 4096
A = 32
L = 128
DEV = 128
BINS = 4
F32 = jnp.float32
BF16 = jnp.bfloat16


def hi_lo(matrix):
    hi = matrix.astype(ml_dtypes.bfloat16)
    lo = (matrix - hi.astype(np.float64)).astype(ml_dtypes.bfloat16)
    return np.stack([hi, lo])


def tables():
    lane = np.arange(L)
    angle = 2.0 * np.pi * ((lane[:, None] * lane[None, :]) % L) / L
    c, s = np.cos(angle), np.sin(angle)
    fwd = np.block([[c, s], [-s, c]])
    slot = np.arange(64)
    a0 = 2.0 * np.pi * ((slot[:, None] * lane[None, :]) % L) / L
    a16 = 2.0 * np.pi * (((16 + 32 * slot[:, None]) * lane[None, :]) % N) / N
    first = np.zeros((256, 256))
    first[0:64, 0:128] = np.cos(a0)
    first[128:192, 0:128] = -np.sin(a0)
    first[128, 0:128] = (-1.0) ** lane
    first[64:128, 128:256] = np.cos(a16)
    first[192:256, 128:256] = -np.sin(a16)
    last = 2.0 * first.copy()
    last[0, 0:128] = 1.0
    last[128, 0:128] = (-1.0) ** lane
    k = np.arange(A)
    tw = 2.0 * np.pi * ((k[:, None] * lane[None, :]) % N) / N
    twid = np.stack([np.cos(tw), np.sin(tw)], 1).astype(np.float32)
    twid = np.broadcast_to(twid[:, :, None, :], (A, 2, 8, L)).copy()
    return dict(
        row=np.stack([hi_lo(first), hi_lo(fwd)]),
        colf=hi_lo(fwd.T),
        coli=hi_lo(fwd),
        back=np.stack([hi_lo(last), hi_lo(fwd)]),
        twid=twid,
    )


def fft(xs, sign):
    n = len(xs)
    if n == 1:
        return xs
    even, odd = fft(xs[0::2], sign), fft(xs[1::2], sign)
    out = [None] * n
    h = n // 2
    root = np.float32(np.sqrt(0.5))
    for k in range(h):
        er, ei = even[k]
        r, i = odd[k]
        if k == 0:
            tr, ti = r, i
        elif 4 * k == n:
            tr, ti = (-i, r) if sign > 0 else (i, -r)
            if sign > 0:
                out[k], out[k + h] = (er - i, ei + r), (er + i, ei - r)
            else:
                out[k], out[k + h] = (er + i, ei - r), (er - i, ei + r)
            continue
        elif 8 * k == n:
            tr, ti = ((r - i) * root, (r + i) * root) if sign > 0 else ((r + i) * root, (i - r) * root)
        elif 8 * k == 3 * n:
            if sign > 0:
                pr, pi = (r + i) * root, (r - i) * root
                out[k], out[k + h] = (er - pr, ei + pi), (er + pr, ei - pi)
            else:
                pr, pi = (i - r) * root, (r + i) * root
                out[k], out[k + h] = (er + pr, ei - pi), (er - pr, ei + pi)
            continue
        else:
            c = np.float32(np.cos(2 * np.pi * k / n))
            s = np.float32(sign * np.sin(2 * np.pi * k / n))
            tr, ti = r * c - i * s, r * s + i * c
        out[k], out[k + h] = (er + tr, ei + ti), (er - tr, ei - ti)
    return out


def rfft(xs):
    n = len(xs)
    if n == 2:
        return [(xs[0] + xs[1], None), (xs[0] - xs[1], None)]
    even, odd = rfft(xs[0::2]), rfft(xs[1::2])
    out = [None] * (n // 2 + 1)
    for k in range(n // 4 + 1):
        if k == 0:
            out[0] = (even[0][0] + odd[0][0], None)
            out[n // 2] = (even[0][0] - odd[0][0], None)
        elif 4 * k == n:
            out[k] = (even[k][0], -odd[k][0])
        else:
            er, ei = even[k]
            r, i = odd[k]
            if 8 * k == n:
                root = np.float32(np.sqrt(0.5))
                tr, ti = (r + i) * root, (i - r) * root
            else:
                c = np.float32(np.cos(2 * np.pi * k / n))
                s = np.float32(np.sin(2 * np.pi * k / n))
                tr, ti = r * c + i * s, i * c - r * s
            out[k] = (er + tr, ei + ti)
            out[n // 2 - k] = (er - tr, ti - ei)
    return out


def irfft(X, n):
    if n == 2:
        a, b = X[0][0], X[1][0]
        return [a + b, a - b]
    h = n // 2
    even, odd = [None] * (h // 2 + 1), [None] * (h // 2 + 1)
    for k in range(h // 2 + 1):
        if k == 0:
            even[0] = (X[0][0] + X[h][0], None)
            odd[0] = (X[0][0] - X[h][0], None)
        elif 2 * k == h:
            even[k] = (X[k][0] + X[k][0], None)
            odd[k] = (-(X[k][1] + X[k][1]), None)
        else:
            ar, ai = X[k]
            br, bi = X[h - k]
            even[k] = (ar + br, ai - bi)
            dr, di = ar - br, ai + bi
            if 4 * k == h:
                root = np.float32(np.sqrt(0.5))
                odd[k] = ((dr - di) * root, (dr + di) * root)
            else:
                c = np.float32(np.cos(2 * np.pi * k / n))
                s = np.float32(np.sin(2 * np.pi * k / n))
                odd[k] = (dr * c - di * s, dr * s + di * c)
    e, o = irfft(even, h), irfft(odd, h)
    out = [None] * n
    out[0::2] = e
    out[1::2] = o
    return out


def split(x):
    hi = x.astype(BF16)
    lo = (x - hi.astype(F32)).astype(BF16)
    return hi, lo


ROWS = 16
STEPS = 128 // ROWS
GROUP = 4
MESH = pl.DeviceIdType.MESH


def mesh_id(device):
    return (device // 32, device % 32)


def row_butterflies(i, x_ref, tw_ref, y_ref):
    for comp in range(2):
        at = pl.ds(pl.multiple_of(8 * i, 8), 8)
        X = rfft([x_ref[comp, at, L * p : L * p + L] for p in range(A)])
        rows = pl.ds(pl.multiple_of(128 * comp + 8 * i, 8), 8)
        y_ref[0, rows, 0:L] = X[0][0]
        y_ref[0, rows, L : 2 * L] = X[16][0]
        for k in range(1, 16):
            r, m = X[k]
            c, s = tw_ref[k, 0], tw_ref[k, 1]
            y_ref[k, rows, 0:L] = r * c + m * s
            y_ref[k, rows, L : 2 * L] = m * c - r * s


def row_matmul(k, w_ref, y_ref, send_ref):
    hi, lo = split(y_ref[k])
    sel = jnp.minimum(k, 1)
    whi, wlo = w_ref[sel, 0], w_ref[sel, 1]
    dims = (((1,), (1,)), ((), ()))
    dot = functools.partial(lax.dot_general, dimension_numbers=dims, preferred_element_type=F32)
    out = dot(whi, hi) + (dot(whi, lo) + dot(wlo, hi))
    for h in range(2):
        for c in range(2):
            for d in range(8):
                at = 128 * c + 64 * h + 8 * d
                send_ref[h, 8 * k + d, c] = out[at : at + 8]


def col_forward(half, b, packed, x_ref, tw_ref, y_ref):
    lane = lax.broadcasted_iota(jnp.int32, (8, L), 1)
    sign = jnp.where(lane % 2 == 0, 1.0, -1.0).astype(F32)
    total = x_ref[half, A * b, 1, :, L : 2 * L]
    for t in range(1, A):
        total = total + x_ref[half, A * b + t, 1, :, L : 2 * L]
    corner = sign * (jnp.sum(total * sign, axis=1, keepdims=True) * np.float32(-1.0 / N))
    for R in range(2):
        xs = []
        for t in range(A):
            re = x_ref[half, A * b + t, 0, :, R * L : R * L + L]
            im = x_ref[half, A * b + t, 1, :, R * L : R * L + L]
            if R == 0:
                im = jnp.where(packed, corner, im)
            else:
                re = jnp.where(packed, 0.0, re)
                im = jnp.where(packed, x_ref[half, A * b + t, 1, :, 0:L], im)
            xs.append((re, im))
        X = fft(xs, -1)
        rows = pl.ds(pl.multiple_of(32 * R + 8 * b, 8), 8)
        for k in range(A):
            r, m = X[k]
            if k:
                c, s = tw_ref[k, 0], tw_ref[k, 1]
                r, m = r * c + m * s, m * c - r * s
            y_ref[k, rows, 0:L] = r
            y_ref[k, rows, L : 2 * L] = m


def col_middle(half, g, me, packed, w, tw_ref, wf_ref, wi_ref, y_ref, z_ref):
    base = g * GROUP
    group, part = me // 8, me % 8
    sub = lax.broadcasted_iota(jnp.int32, (8, L), 0)
    lane = lax.broadcasted_iota(jnp.int32, (8, L), 1)
    hi, lo = split(y_ref[pl.ds(base, GROUP)].reshape(GROUP * 64, 256))
    dot = functools.partial(jnp.dot, preferred_element_type=F32)
    G = dot(hi, wf_ref[0]) + (dot(lo, wf_ref[0]) + dot(hi, wf_ref[1]))
    at = 8 * part + sub
    col = jnp.where(group == 0, 32 * at + 16 * half, group + 32 * (64 * half + at))
    col = jnp.where(col < N // 2, col, col - N).astype(F32)
    rows = []
    for kk in range(GROUP):
        u = base + kk + A * lane
        nyquist = u == N // 2
        row = jnp.where(u < N // 2, u, u - N).astype(F32)
        row2 = row * row

        def kern(l1):
            q = jnp.maximum(l1 * l1 + row2, 1.0)
            return (l1 * l1 - row2) / q, (2.0 * l1) * row / q

        a, b = kern(col)
        ar, ai = a, jnp.where(nyquist, -b, 0.0)
        a2, b2 = kern(np.float32(-N // 2))
        br = jnp.where(packed, a2, jnp.where(nyquist, 0.0, b))
        bi = jnp.where(jnp.logical_and(packed, jnp.logical_not(nyquist)), -b2, 0.0)
        H = []
        for b_ in range(BINS):
            o1, o2 = kk * 64 + 8 * b_, kk * 64 + 32 + 8 * b_
            g1r, g1i = G[o1 : o1 + 8, 0:L], G[o1 : o1 + 8, L : 2 * L]
            g2r, g2i = G[o2 : o2 + 8, 0:L], G[o2 : o2 + 8, L : 2 * L]
            hr = ar * g1r - ai * g1i + br * g2r - bi * g2i
            hm = ar * g1i + ai * g1r + br * g2i + bi * g2r
            H.append((hr, hm))
        for j in range(BINS):
            fr, fi = H[0][0] * w[j][0], H[0][1] * w[j][0]
            for b_ in range(1, j + 1):
                fr, fi = fr + H[b_][0] * w[j][b_], fi + H[b_][1] * w[j][b_]
            rows.append(jnp.concatenate([fr, fi], axis=1))
    hi, lo = split(jnp.concatenate(rows, axis=0))
    Z = dot(hi, wi_ref[0]) + (dot(lo, wi_ref[0]) + dot(hi, wi_ref[1]))
    for kk in range(GROUP):
        c, s = tw_ref[base + kk, 0], tw_ref[base + kk, 1]
        for j in range(BINS):
            o = 32 * kk + 8 * j
            r, m = Z[o : o + 8, 0:L], Z[o : o + 8, L : 2 * L]
            z_ref[base + kk, 8 * j : 8 * j + 8, 0:L] = r * c - m * s
            z_ref[base + kk, 8 * j : 8 * j + 8, L : 2 * L] = m * c + r * s


def col_inverse(half, j, z_ref, ret_ref):
    rows = pl.ds(pl.multiple_of(8 * j, 8), 8)
    xs = [(z_ref[k, rows, 0:L], z_ref[k, rows, L : 2 * L]) for k in range(A)]
    for t, (r, m) in enumerate(fft(xs, 1)):
        ret_ref[half, A * j + t, 0] = r
        ret_ref[half, A * j + t, 1] = m


def main_kernel(
    wgt_ref, g1_ref, g2_ref, tw_ref, wr_ref, wf_ref, wi_ref, out_ref,
    x_ref, yr_ref, send_ref, recv_ref, y_ref, z_ref, ret_ref,
    in_sem, go_send, go_recv, ret_send, ret_recv, own_sem,
):
    me = lax.axis_index("bin") * 32 + lax.axis_index("tile")

    barrier = pltpu.get_barrier_semaphore()

    def greet(i, carry):
        pl.semaphore_signal(
            barrier, inc=1, device_id=mesh_id((me + i) % DEV), device_id_type=MESH
        )
        return carry

    lax.fori_loop(1, DEV, greet, 0)

    def load(comp, i):
        rows = pl.ds(pl.multiple_of(8 * i, 8), 8)
        return pltpu.make_async_copy(
            (g1_ref, g2_ref)[comp].at[rows], x_ref.at[comp, rows], in_sem.at[comp, i]
        )

    def start_load(i, carry):
        load(0, i).start()
        load(1, i).start()
        return carry

    lax.fori_loop(0, 16, start_load, 0)

    def rows_step(i, carry):
        load(0, i).wait()
        load(1, i).wait()
        row_butterflies(i, x_ref, tw_ref, yr_ref)
        return carry

    lax.fori_loop(0, 16, rows_step, 0)
    pl.semaphore_wait(barrier, DEV - 1)

    def go(half, dest):
        @pl.when(dest != me)
        def _():
            pltpu.make_async_remote_copy(
                src_ref=send_ref.at[half, dest],
                dst_ref=recv_ref.at[half, me],
                send_sem=go_send.at[half],
                recv_sem=go_recv.at[half],
                device_id=mesh_id(dest),
                device_id_type=MESH,
            ).start()

    def go_own(half):
        return pltpu.make_async_copy(
            send_ref.at[half, me], recv_ref.at[half, me], own_sem.at[half]
        )

    def matmul_step(i, carry):
        k = (me // 8 + i) % 16
        row_matmul(k, wr_ref, yr_ref, send_ref)
        for e in range(8):
            go(0, 8 * k + (me + e) % 8)
        return carry

    lax.fori_loop(0, 16, matmul_step, 0)
    go_own(0).start()
    go_own(1).start()

    def second(i, carry):
        go(1, 8 * ((me // 8 + i // 8) % 16) + (me + i) % 8)
        return carry

    lax.fori_loop(0, DEV, second, 0)

    sub = lax.broadcasted_iota(jnp.int32, (8, L), 0)
    scale = np.float32(1.0 / (N * N))
    w = [[wgt_ref[j, b] * scale for b in range(j + 1)] for j in range(BINS)]

    def all_but_one(src, dst, send, recv, half):
        return pltpu.make_async_remote_copy(
            src_ref=src.at[half, pl.ds(0, DEV - 1)],
            dst_ref=dst.at[half, pl.ds(0, DEV - 1)],
            send_sem=send.at[half],
            recv_sem=recv.at[half],
            device_id=mesh_id(me),
            device_id_type=MESH,
        )

    def ret_own(half):
        return pltpu.make_async_copy(
            ret_ref.at[half, me], out_ref.at[half, me], own_sem.at[2 + half]
        )

    def half_step(half, carry):
        packed = jnp.logical_and(sub == 0, jnp.logical_and(me == 0, half == 0))
        go_own(half).wait()
        all_but_one(send_ref, recv_ref, go_send, go_recv, half).wait_recv()

        def forward(b, c):
            col_forward(half, b, packed, recv_ref, tw_ref, y_ref)
            return c

        def middle(g, c):
            col_middle(half, g, me, packed, w, tw_ref, wf_ref, wi_ref, y_ref, z_ref)
            return c

        def inverse(i, c):
            j = (me // 32 + i) % BINS
            col_inverse(half, j, z_ref, ret_ref)

            def ret(e, c2):
                dest = 32 * j + (me + e) % 32

                @pl.when(dest != me)
                def _():
                    pltpu.make_async_remote_copy(
                        src_ref=ret_ref.at[half, dest],
                        dst_ref=out_ref.at[half, me],
                        send_sem=ret_send.at[half],
                        recv_sem=ret_recv.at[half],
                        device_id=mesh_id(dest),
                        device_id_type=MESH,
                    ).start()

                return c2

            return lax.fori_loop(0, 32, ret, c)

        lax.fori_loop(0, BINS, forward, 0)
        lax.fori_loop(0, A // GROUP, middle, 0)
        lax.fori_loop(0, BINS, inverse, 0)
        ret_own(half).start()
        return carry

    lax.fori_loop(0, 2, half_step, 0)

    def finish(half, carry):
        all_but_one(send_ref, recv_ref, go_send, go_recv, half).wait_send()
        all_but_one(ret_ref, out_ref, ret_send, ret_recv, half).wait_send()
        all_but_one(ret_ref, out_ref, ret_send, ret_recv, half).wait_recv()
        ret_own(half).wait()
        return carry

    lax.fori_loop(0, 2, finish, 0)


def main_stage(g1, g2, weights, tab):
    vmem = pl.BlockSpec(memory_space=pltpu.VMEM)
    hbm = pl.BlockSpec(memory_space=pl.ANY)
    return pl.pallas_call(
        main_kernel,
        in_specs=[pl.BlockSpec(memory_space=pltpu.SMEM), hbm, hbm, vmem, vmem, vmem, vmem],
        out_specs=hbm,
        out_shape=jax.ShapeDtypeStruct((2, DEV, 2, 8, L), F32),
        scratch_shapes=[
            pltpu.VMEM((2, 128, N), F32),
            pltpu.VMEM((16, 256, 256), F32),
            pltpu.VMEM((2, DEV, 2, 8, 256), F32),
            pltpu.VMEM((2, DEV, 2, 8, 256), F32),
            pltpu.VMEM((A, 64, 256), F32),
            pltpu.VMEM((A, 32, 256), F32),
            pltpu.VMEM((2, DEV, 2, 8, L), F32),
            pltpu.SemaphoreType.DMA((2, 16)),
            pltpu.SemaphoreType.DMA((2,)),
            pltpu.SemaphoreType.DMA((2,)),
            pltpu.SemaphoreType.DMA((2,)),
            pltpu.SemaphoreType.DMA((2,)),
            pltpu.SemaphoreType.DMA((4,)),
        ],
        compiler_params=pltpu.CompilerParams(
            collective_id=0, has_side_effects=True, vmem_limit_bytes=62 * 2**20
        ),
        name="main",
    )(weights, g1.reshape(128, N), g2.reshape(128, N), tab["twid"], tab["row"], tab["colf"], tab["coli"])


def back_kernel(x_ref, tw_ref, w_ref, out_ref, z_ref):
    i = pl.program_id(0)

    @pl.when(i < 16)
    def _():
        parts = [x_ref[h, d, c] for c in range(2) for h in range(2) for d in range(8)]
        hi, lo = split(jnp.concatenate(parts, axis=0).T)
        sel = jnp.minimum(i, 1)
        dot = functools.partial(jnp.dot, preferred_element_type=F32)
        Z = dot(hi, w_ref[sel, 0]) + (dot(lo, w_ref[sel, 0]) + dot(hi, w_ref[sel, 1]))
        c, s = tw_ref[i, 0, 0:1], tw_ref[i, 1, 0:1]
        r, m = Z[:, 0:L], Z[:, L : 2 * L]
        z_ref[i, :, 0:L] = r * c - m * s
        z_ref[i, :, L : 2 * L] = m * c + r * s

    @pl.when(i >= 16)
    def _():
        for j in range(ROWS // 8):
            rows = pl.ds(pl.multiple_of((i - 16) * ROWS + 8 * j, 8), 8)
            X = [(z_ref[0, rows, 0:L], None)]
            X += [(z_ref[k, rows, 0:L], z_ref[k, rows, L : 2 * L]) for k in range(1, 16)]
            X += [(z_ref[0, rows, L : 2 * L], None)]
            for p, v in enumerate(irfft(X, A)):
                out_ref[8 * j : 8 * j + 8, L * p : L * p + L] = v


def back_stage(x, tab):
    return pl.pallas_call(
        back_kernel,
        grid=(16 + STEPS,),
        in_specs=[
            pl.BlockSpec((2, 8, 2, 8, L), lambda i: (0, jnp.minimum(i, 15), 0, 0, 0)),
            pl.BlockSpec((A, 2, 8, L), lambda i: (0, 0, 0, 0)),
            pl.BlockSpec((2, 2, 256, 256), lambda i: (0, 0, 0, 0)),
        ],
        out_specs=pl.BlockSpec((ROWS, N), lambda i: (jnp.maximum(i - 16, 0), 0)),
        out_shape=jax.ShapeDtypeStruct((128, N), F32),
        scratch_shapes=[pltpu.VMEM((16, 128, 256), F32)],
        name="back",
    )(x, tab["twid"], tab["back"])


def on_device(shear_one, shear_two, weights):
    tab = {k: jnp.asarray(v) for k, v in tables().items()}
    x = main_stage(shear_one, shear_two, weights, tab)
    return back_stage(x, tab).reshape(1, 128, N)


def solution(mesh):
    spec = P("bin", "tile", None)
    return jax.shard_map(
        on_device, mesh=mesh, in_specs=(spec, spec, P()), out_specs=spec, check_vma=False
    )
```

time: 153 us -> 108 us (0.71)
  blocking collectives: 66 us -> 0 us
  Pallas kernels: 47.2 us -> 108 us
  waiting for transfers between devices: 29.8 us -> 0 us
  starting transfers between devices: 8.84 us -> 0 us
    all_to_all x2 -> x0, blocking collectives: 66 us -> none  [exchange(): lax.all_to_all(x, ('bin', 'tile'), split_axis=0, concat_axis=0, tiled=True)]
    pallas_call x4 -> x2, Pallas kernels: 47.2 us -> 108 us  [the longest x1 94.5 us: main_stage(): pl.pallas_call(main_kernel, in_specs=[pl.BlockSpec(memory_space=pltpu.SME...]
    all_to_all x2 -> x0, waiting for transfers between devices: 29.8 us -> none  [exchange(): lax.all_to_all(x, ('bin', 'tile'), split_axis=0, concat_axis=0, tiled=True)]
    all_to_all x2 -> x0, starting transfers between devices: 8.84 us -> none  [exchange(): lax.all_to_all(x, ('bin', 'tile'), split_axis=0, concat_axis=0, tiled=True)]
  transfers between devices with their start and end apart: 2 -> 0, of which waited for: 2 -> 0; matrix products, arithmetic and copies ran while one was open for 0% -> 0% of each run, Pallas kernels for 13% -> 0%
where the time goes in v1:
time: 108 us
  Pallas kernels  108 us (100%)
    pallas_call x1, Pallas kernels, main_stage(): pl.pallas_call(main_kernel, in_specs=[pl.BlockSpec(memory_space=pltpu.SME...  94.5 us
    pallas_call x1, Pallas kernels, back_stage(): pl.pallas_call(back_kernel, grid=(16 + STEPS,), in_specs=[pl.BlockSpec((2...  13.6 us

profile of v1, /device:TPU:1, one launch (start us, length us, event | category | flops | bytes accessed | tf_op | source)
XLA Modules:
  0.0 108.1 jit_solution(10337130483688880524)
XLA Ops:
  0.0 94.5 %main.1.x_ref = f32[2,128,2,8,128]{4,3,2,1,0:T(8,128)} custom-call(f32[4,4]{1,0:T(4,128)} %wgt_ref.1, f32[128,4096]{1,0:T(8,128)} %bitcast.3, f32[128,4096]{1,0:T(8,128)} %bitcast.4, f32[32,2,8,128]{3,2,1,0:T(8,128)} %constant.14.clone.tw_ref, bf16[2,2,256,256]{3,2,1,0:T(8,128)(2,1)} %constant.10.clone.wr_ref, bf16[2,256,256]{2,1,0:T(8,128)(2,1)} %constant.11.clone.wf_ref, ...), custom_call_target="tpu_custom_call" | custom-call | tf_op jit(solution)/shard_map/main/pallas_call | solution.py:434
  94.5 13.6 %back.1 = f32[128,4096]{1,0:T(8,128)} custom-call(f32[2,128,2,8,128]{4,3,2,1,0:T(8,128)} %main.1.x_ref, f32[32,2,8,128]{3,2,1,0:T(8,128)} %constant.14.clone.tw_ref, bf16[2,2,256,256]{3,2,1,0:T(8,128)(2,1)} %constant.13.clone.w_ref), custom_call_target="tpu_custom_call" | custom-call | tf_op jit(solution)/shard_map/back/pallas_call | solution.py:488

commit v2 on v1

--- a/solution.py
+++ b/solution.py
@@ -160,28 +160,22 @@
 ROWS = 16
 STEPS = 128 // ROWS
 GROUP = 4
-MESH = pl.DeviceIdType.MESH
-
-
-def mesh_id(device):
-    return (device // 32, device % 32)
-
-
-def row_butterflies(i, x_ref, tw_ref, y_ref):
-    for comp in range(2):
-        at = pl.ds(pl.multiple_of(8 * i, 8), 8)
-        X = rfft([x_ref[comp, at, L * p : L * p + L] for p in range(A)])
-        rows = pl.ds(pl.multiple_of(128 * comp + 8 * i, 8), 8)
-        y_ref[0, rows, 0:L] = X[0][0]
-        y_ref[0, rows, L : 2 * L] = X[16][0]
-        for k in range(1, 16):
-            r, m = X[k]
-            c, s = tw_ref[k, 0], tw_ref[k, 1]
-            y_ref[k, rows, 0:L] = r * c + m * s
-            y_ref[k, rows, L : 2 * L] = m * c - r * s
-
-
-def row_matmul(k, w_ref, y_ref, send_ref):
+FLAT = pl.DeviceIdType.LOGICAL
+
+
+def row_butterflies(comp, i, x_ref, tw_ref, y_ref):
+    rows = pl.ds(pl.multiple_of(8 * i, 8), 8)
+    X = rfft([x_ref[comp, rows, L * p : L * p + L] for p in range(A)])
+    y_ref[0, rows, 0:L] = X[0][0]
+    y_ref[0, rows, L : 2 * L] = X[16][0]
+    for k in range(1, 16):
+        r, m = X[k]
+        c, s = tw_ref[k, 0], tw_ref[k, 1]
+        y_ref[k, rows, 0:L] = r * c + m * s
+        y_ref[k, rows, L : 2 * L] = m * c - r * s
+
+
+def row_matmul(comp, k, w_ref, y_ref, send_ref):
     hi, lo = split(y_ref[k])
     sel = jnp.minimum(k, 1)
     whi, wlo = w_ref[sel, 0], w_ref[sel, 1]
@@ -192,26 +186,26 @@
         for c in range(2):
             for d in range(8):
                 at = 128 * c + 64 * h + 8 * d
-                send_ref[h, 8 * k + d, c] = out[at : at + 8]
+                send_ref[h, 8 * k + d, comp, c] = out[at : at + 8]
 
 
 def col_forward(half, b, packed, x_ref, tw_ref, y_ref):
     lane = lax.broadcasted_iota(jnp.int32, (8, L), 1)
     sign = jnp.where(lane % 2 == 0, 1.0, -1.0).astype(F32)
-    total = x_ref[half, A * b, 1, :, L : 2 * L]
+    total = x_ref[half, A * b, 1, 1]
     for t in range(1, A):
-        total = total + x_ref[half, A * b + t, 1, :, L : 2 * L]
+        total = total + x_ref[half, A * b + t, 1, 1]
     corner = sign * (jnp.sum(total * sign, axis=1, keepdims=True) * np.float32(-1.0 / N))
     for R in range(2):
         xs = []
         for t in range(A):
-            re = x_ref[half, A * b + t, 0, :, R * L : R * L + L]
-            im = x_ref[half, A * b + t, 1, :, R * L : R * L + L]
+            re = x_ref[half, A * b + t, R, 0]
+            im = x_ref[half, A * b + t, R, 1]
             if R == 0:
                 im = jnp.where(packed, corner, im)
             else:
                 re = jnp.where(packed, 0.0, re)
-                im = jnp.where(packed, x_ref[half, A * b + t, 1, :, 0:L], im)
+                im = jnp.where(packed, x_ref[half, A * b + t, 0, 1], im)
             xs.append((re, im))
         X = fft(xs, -1)
         rows = pl.ds(pl.multiple_of(32 * R + 8 * b, 8), 8)
@@ -283,102 +277,122 @@
         ret_ref[half, A * j + t, 1] = m
 
 
+def back_matmul(k, in_ref, tw_ref, w_ref, z_ref):
+    parts = [in_ref[h, 8 * k + d, c] for c in range(2) for h in range(2) for d in range(8)]
+    hi, lo = split(jnp.concatenate(parts, axis=0).T)
+    sel = jnp.minimum(k, 1)
+    dot = functools.partial(jnp.dot, preferred_element_type=F32)
+    Z = dot(hi, w_ref[sel, 0]) + (dot(lo, w_ref[sel, 0]) + dot(hi, w_ref[sel, 1]))
+    c, s = tw_ref[k, 0, 0:1], tw_ref[k, 1, 0:1]
+    r, m = Z[:, 0:L], Z[:, L : 2 * L]
+    z_ref[k, :, 0:L] = r * c - m * s
+    z_ref[k, :, L : 2 * L] = m * c + r * s
+
+
 def main_kernel(
-    wgt_ref, g1_ref, g2_ref, tw_ref, wr_ref, wf_ref, wi_ref, out_ref,
-    x_ref, yr_ref, send_ref, recv_ref, y_ref, z_ref, ret_ref,
-    in_sem, go_send, go_recv, ret_send, ret_recv, own_sem,
+    wgt_ref, g1_ref, g2_ref, tw_any, wr_any, wf_any, wi_any, wb_any, out_ref,
+    tw_ref, wr_ref, wf_ref, wi_ref, wb_ref,
+    x_ref, yr_ref, send_ref, recv_ref, y_ref, z_ref, ret_ref, land_ref, last_ref,
+    tab_sem, in_sem, go_send, go_recv, ret_send, ret_recv, out_sem,
 ):
-    me = lax.axis_index("bin") * 32 + lax.axis_index("tile")
+    mybin, mytile = lax.axis_index("bin"), lax.axis_index("tile")
+    me = mybin * 32 + mytile
+    mygroup, mypart = mybin * 4 + lax.div(mytile, 8), lax.rem(mytile, 8)
 
     barrier = pltpu.get_barrier_semaphore()
 
     def greet(i, carry):
         pl.semaphore_signal(
-            barrier, inc=1, device_id=mesh_id((me + i) % DEV), device_id_type=MESH
+            barrier, inc=1, device_id=lax.rem(me + i, DEV), device_id_type=FLAT
         )
         return carry
 
-    lax.fori_loop(1, DEV, greet, 0)
+    tabs = [
+        pltpu.make_async_copy(a, b, tab_sem.at[i])
+        for i, (a, b) in enumerate(
+            zip((tw_any, wr_any, wf_any, wi_any, wb_any), (tw_ref, wr_ref, wf_ref, wi_ref, wb_ref))
+        )
+    ]
 
     def load(comp, i):
-        rows = pl.ds(pl.multiple_of(8 * i, 8), 8)
+        rows = pl.ds(pl.multiple_of(32 * i, 32), 32)
         return pltpu.make_async_copy(
             (g1_ref, g2_ref)[comp].at[rows], x_ref.at[comp, rows], in_sem.at[comp, i]
         )
 
-    def start_load(i, carry):
+    tabs[0].start()
+    for i in range(4):
         load(0, i).start()
+    tabs[1].start()
+    for i in range(4):
         load(1, i).start()
+    for t in tabs[2:]:
+        t.start()
+    lax.fori_loop(1, DEV, greet, 0)
+    tabs[0].wait()
+
+    def go(half, dest, comp):
+        at = (half, dest) if comp is None else (half, dest, comp)
+        to = (half, me) if comp is None else (half, me, comp)
+        pltpu.make_async_remote_copy(
+            src_ref=send_ref.at[at],
+            dst_ref=recv_ref.at[to],
+            send_sem=go_send.at[half],
+            recv_sem=go_recv.at[half],
+            device_id=dest,
+            device_id_type=FLAT,
+        ).start()
+
+    def rows_of(comp):
+        def some_rows(i, carry):
+            load(comp, i).wait()
+
+            def step(j, c):
+                row_butterflies(comp, 4 * i + j, x_ref, tw_ref, yr_ref)
+                return c
+
+            return lax.fori_loop(0, 4, step, carry)
+
+        def matmul_step(i, carry):
+            k = lax.rem(mygroup + i, 16)
+            row_matmul(comp, k, wr_ref, yr_ref, send_ref)
+
+            @pl.when(i > 0)
+            def _():
+                go(0, 8 * k + mypart, comp)
+
+            for e in range(1, 8):
+                go(0, 8 * k + lax.rem(mypart + e, 8), comp)
+            return carry
+
+        lax.fori_loop(0, 4, some_rows, 0)
+        if comp == 0:
+            tabs[1].wait()
+            pl.semaphore_wait(barrier, DEV - 1)
+        lax.fori_loop(0, 16, matmul_step, 0)
+
+    rows_of(0)
+    rows_of(1)
+    for half in range(2):
+        pltpu.make_async_copy(
+            send_ref.at[half, me], recv_ref.at[half, me], go_recv.at[half]
+        ).start()
+
+    def second(i, carry):
+        go(1, 8 * lax.rem(mygroup + lax.div(i, 8), 16) + lax.rem(mypart + i, 8), None)
         return carry
 
-    lax.fori_loop(0, 16, start_load, 0)
-
-    def rows_step(i, carry):
-        load(0, i).wait()
-        load(1, i).wait()
-        row_butterflies(i, x_ref, tw_ref, yr_ref)
-        return carry
-
-    lax.fori_loop(0, 16, rows_step, 0)
-    pl.semaphore_wait(barrier, DEV - 1)
-
-    def go(half, dest):
-        @pl.when(dest != me)
-        def _():
-            pltpu.make_async_remote_copy(
-                src_ref=send_ref.at[half, dest],
-                dst_ref=recv_ref.at[half, me],
-                send_sem=go_send.at[half],
-                recv_sem=go_recv.at[half],
-                device_id=mesh_id(dest),
-                device_id_type=MESH,
-            ).start()
-
-    def go_own(half):
-        return pltpu.make_async_copy(
-            send_ref.at[half, me], recv_ref.at[half, me], own_sem.at[half]
-        )
-
-    def matmul_step(i, carry):
-        k = (me // 8 + i) % 16
-        row_matmul(k, wr_ref, yr_ref, send_ref)
-        for e in range(8):
-            go(0, 8 * k + (me + e) % 8)
-        return carry
-
-    lax.fori_loop(0, 16, matmul_step, 0)
-    go_own(0).start()
-    go_own(1).start()
-
-    def second(i, carry):
-        go(1, 8 * ((me // 8 + i // 8) % 16) + (me + i) % 8)
-        return carry
-
-    lax.fori_loop(0, DEV, second, 0)
+    lax.fori_loop(1, DEV, second, 0)
+    for t in tabs[2:]:
+        t.wait()
 
     sub = lax.broadcasted_iota(jnp.int32, (8, L), 0)
     scale = np.float32(1.0 / (N * N))
     w = [[wgt_ref[j, b] * scale for b in range(j + 1)] for j in range(BINS)]
 
-    def all_but_one(src, dst, send, recv, half):
-        return pltpu.make_async_remote_copy(
-            src_ref=src.at[half, pl.ds(0, DEV - 1)],
-            dst_ref=dst.at[half, pl.ds(0, DEV - 1)],
-            send_sem=send.at[half],
-            recv_sem=recv.at[half],
-            device_id=mesh_id(me),
-            device_id_type=MESH,
-        )
-
-    def ret_own(half):
-        return pltpu.make_async_copy(
-            ret_ref.at[half, me], out_ref.at[half, me], own_sem.at[2 + half]
-        )
-
     def half_step(half, carry):
         packed = jnp.logical_and(sub == 0, jnp.logical_and(me == 0, half == 0))
-        go_own(half).wait()
-        all_but_one(send_ref, recv_ref, go_send, go_recv, half).wait_recv()
+        pltpu.make_async_copy(send_ref.at[half], recv_ref.at[half], go_recv.at[half]).wait()
 
         def forward(b, c):
             col_forward(half, b, packed, recv_ref, tw_ref, y_ref)
@@ -389,121 +403,141 @@
             return c
 
         def inverse(i, c):
-            j = (me // 32 + i) % BINS
+            j = lax.rem(mybin + i, BINS)
             col_inverse(half, j, z_ref, ret_ref)
 
-            def ret(e, c2):
-                dest = 32 * j + (me + e) % 32
-
-                @pl.when(dest != me)
-                def _():
-                    pltpu.make_async_remote_copy(
-                        src_ref=ret_ref.at[half, dest],
-                        dst_ref=out_ref.at[half, me],
-                        send_sem=ret_send.at[half],
-                        recv_sem=ret_recv.at[half],
-                        device_id=mesh_id(dest),
-                        device_id_type=MESH,
-                    ).start()
-
+            def ret(dest):
+                pltpu.make_async_remote_copy(
+                    src_ref=ret_ref.at[half, dest],
+                    dst_ref=land_ref.at[half, me],
+                    send_sem=ret_send.at[half],
+                    recv_sem=ret_recv.at[half, mygroup],
+                    device_id=dest,
+                    device_id_type=FLAT,
+                ).start()
+
+            def ret_step(e, c2):
+                z = lax.rem(lax.div(mytile, 8) + lax.div(e, 8), 4)
+                ret(32 * j + 8 * z + lax.rem(mypart + e, 8))
                 return c2
 
-            return lax.fori_loop(0, 32, ret, c)
+            @pl.when(i > 0)
+            def _():
+                ret(32 * j + mytile)
+
+            return lax.fori_loop(1, 32, ret_step, c)
 
         lax.fori_loop(0, BINS, forward, 0)
         lax.fori_loop(0, A // GROUP, middle, 0)
         lax.fori_loop(0, BINS, inverse, 0)
-        ret_own(half).start()
+        pltpu.make_async_copy(
+            ret_ref.at[half, me], land_ref.at[half, me], ret_recv.at[half, mygroup]
+        ).start()
         return carry
 
     lax.fori_loop(0, 2, half_step, 0)
 
+    def write(k):
+        return pltpu.make_async_copy(last_ref.at[k], out_ref.at[k], out_sem.at[k])
+
+    def back_step(i, carry):
+        b = lax.rem(mybin + 4 - lax.div(i, 4), 4)
+        z = lax.rem(lax.div(mytile, 8) + 4 - lax.rem(i, 4), 4)
+        k = 4 * b + z
+        eight = pl.ds(pl.multiple_of(8 * k, 8), 8)
+        for half in range(2):
+            pltpu.make_async_copy(
+                ret_ref.at[half, eight], land_ref.at[half, eight], ret_recv.at[half, k]
+            ).wait()
+        back_matmul(k, land_ref, tw_ref, wb_ref, last_ref)
+        write(k).start()
+        return carry
+
+    lax.fori_loop(0, 16, back_step, 0)
+
     def finish(half, carry):
-        all_but_one(send_ref, recv_ref, go_send, go_recv, half).wait_send()
-        all_but_one(ret_ref, out_ref, ret_send, ret_recv, half).wait_send()
-        all_but_one(ret_ref, out_ref, ret_send, ret_recv, half).wait_recv()
-        ret_own(half).wait()
+        for src, sem in ((send_ref, go_send), (ret_ref, ret_send)):
+            part = src.at[half, pl.ds(0, DEV - 1)]
+            pltpu.make_async_remote_copy(
+                src_ref=part, dst_ref=part, send_sem=sem.at[half], recv_sem=sem.at[half],
+                device_id=me, device_id_type=FLAT,
+            ).wait_send()
         return carry
 
     lax.fori_loop(0, 2, finish, 0)
 
+    def written(k, carry):
+        write(k).wait()
+        return carry
+
+    lax.fori_loop(0, 16, written, 0)
+
 
 def main_stage(g1, g2, weights, tab):
-    vmem = pl.BlockSpec(memory_space=pltpu.VMEM)
     hbm = pl.BlockSpec(memory_space=pl.ANY)
     return pl.pallas_call(
         main_kernel,
-        in_specs=[pl.BlockSpec(memory_space=pltpu.SMEM), hbm, hbm, vmem, vmem, vmem, vmem],
+        in_specs=[pl.BlockSpec(memory_space=pltpu.SMEM)] + [hbm] * 7,
         out_specs=hbm,
-        out_shape=jax.ShapeDtypeStruct((2, DEV, 2, 8, L), F32),
+        out_shape=jax.ShapeDtypeStruct((16, 128, 256), F32),
         scratch_shapes=[
+            pltpu.VMEM((A, 2, 8, L), F32),
+            pltpu.VMEM((2, 2, 256, 256), BF16),
+            pltpu.VMEM((2, 256, 256), BF16),
+            pltpu.VMEM((2, 256, 256), BF16),
+            pltpu.VMEM((2, 2, 256, 256), BF16),
             pltpu.VMEM((2, 128, N), F32),
-            pltpu.VMEM((16, 256, 256), F32),
-            pltpu.VMEM((2, DEV, 2, 8, 256), F32),
-            pltpu.VMEM((2, DEV, 2, 8, 256), F32),
+            pltpu.VMEM((16, 128, 256), F32),
+            pltpu.VMEM((2, DEV, 2, 2, 8, L), F32),
+            pltpu.VMEM((2, DEV, 2, 2, 8, L), F32),
             pltpu.VMEM((A, 64, 256), F32),
             pltpu.VMEM((A, 32, 256), F32),
             pltpu.VMEM((2, DEV, 2, 8, L), F32),
-            pltpu.SemaphoreType.DMA((2, 16)),
+            pltpu.VMEM((2, DEV, 2, 8, L), F32),
+            pltpu.VMEM((16, 128, 256), F32),
+            pltpu.SemaphoreType.DMA((5,)),
+            pltpu.SemaphoreType.DMA((2, 4)),
             pltpu.SemaphoreType.DMA((2,)),
             pltpu.SemaphoreType.DMA((2,)),
             pltpu.SemaphoreType.DMA((2,)),
-            pltpu.SemaphoreType.DMA((2,)),
-            pltpu.SemaphoreType.DMA((4,)),
+            pltpu.SemaphoreType.DMA((2, 16)),
+            pltpu.SemaphoreType.DMA((16,)),
         ],
         compiler_params=pltpu.CompilerParams(
             collective_id=0, has_side_effects=True, vmem_limit_bytes=62 * 2**20
         ),
         name="main",
-    )(weights, g1.reshape(128, N), g2.reshape(128, N), tab["twid"], tab["row"], tab["colf"], tab["coli"])
-
-
-def back_kernel(x_ref, tw_ref, w_ref, out_ref, z_ref):
-    i = pl.program_id(0)
-
-    @pl.when(i < 16)
-    def _():
-        parts = [x_ref[h, d, c] for c in range(2) for h in range(2) for d in range(8)]
-        hi, lo = split(jnp.concatenate(parts, axis=0).T)
-        sel = jnp.minimum(i, 1)
-        dot = functools.partial(jnp.dot, preferred_element_type=F32)
-        Z = dot(hi, w_ref[sel, 0]) + (dot(lo, w_ref[sel, 0]) + dot(hi, w_ref[sel, 1]))
-        c, s = tw_ref[i, 0, 0:1], tw_ref[i, 1, 0:1]
-        r, m = Z[:, 0:L], Z[:, L : 2 * L]
-        z_ref[i, :, 0:L] = r * c - m * s
-        z_ref[i, :, L : 2 * L] = m * c + r * s
-
-    @pl.when(i >= 16)
-    def _():
-        for j in range(ROWS // 8):
-            rows = pl.ds(pl.multiple_of((i - 16) * ROWS + 8 * j, 8), 8)
-            X = [(z_ref[0, rows, 0:L], None)]
-            X += [(z_ref[k, rows, 0:L], z_ref[k, rows, L : 2 * L]) for k in range(1, 16)]
-            X += [(z_ref[0, rows, L : 2 * L], None)]
-            for p, v in enumerate(irfft(X, A)):
-                out_ref[8 * j : 8 * j + 8, L * p : L * p + L] = v
-
-
-def back_stage(x, tab):
+    )(
+        weights, g1.reshape(128, N), g2.reshape(128, N),
+        tab["twid"], tab["row"], tab["colf"], tab["coli"], tab["back"],
+    )
+
+
+def last_kernel(z_ref, out_ref):
+    for j in range(ROWS // 8):
+        rows = slice(8 * j, 8 * j + 8)
+        X = [(z_ref[0, rows, 0:L], None)]
+        X += [(z_ref[k, rows, 0:L], z_ref[k, rows, L : 2 * L]) for k in range(1, 16)]
+        X += [(z_ref[0, rows, L : 2 * L], None)]
+        for p, v in enumerate(irfft(X, A)):
+            out_ref[rows, L * p : L * p + L] = v
+
+
+def last_stage(z):
     return pl.pallas_call(
-        back_kernel,
-        grid=(16 + STEPS,),
-        in_specs=[
-            pl.BlockSpec((2, 8, 2, 8, L), lambda i: (0, jnp.minimum(i, 15), 0, 0, 0)),
-            pl.BlockSpec((A, 2, 8, L), lambda i: (0, 0, 0, 0)),
-            pl.BlockSpec((2, 2, 256, 256), lambda i: (0, 0, 0, 0)),
-        ],
-        out_specs=pl.BlockSpec((ROWS, N), lambda i: (jnp.maximum(i - 16, 0), 0)),
+        last_kernel,
+        grid=(STEPS,),
+        in_specs=[pl.BlockSpec((16, ROWS, 256), lambda i: (0, i, 0))],
+        out_specs=pl.BlockSpec((ROWS, N), lambda i: (i, 0)),
         out_shape=jax.ShapeDtypeStruct((128, N), F32),
-        scratch_shapes=[pltpu.VMEM((16, 128, 256), F32)],
-        name="back",
-    )(x, tab["twid"], tab["back"])
+        name="last",
+    )(z)
 
 
 def on_device(shear_one, shear_two, weights):
     tab = {k: jnp.asarray(v) for k, v in tables().items()}
-    x = main_stage(shear_one, shear_two, weights, tab)
-    return back_stage(x, tab).reshape(1, 128, N)
+    z = main_stage(shear_one, shear_two, weights, tab)
+    return last_stage(z).reshape(1, 128, N)
 
 
 def solution(mesh):

time: 108 us -> 92.2 us (0.85)
  Pallas kernels: 108 us -> 91.9 us
    pallas_call x1, Pallas kernels: 94.5 us -> 86 us  [main_stage(): pl.pallas_call(main_kernel, in_specs=[pl.BlockSpec(memory_space=pltpu.SME...]
    pallas_call x1, Pallas kernels: 13.6 us -> 5.88 us  [last_stage(): pl.pallas_call(last_kernel, grid=(STEPS,), in_specs=[pl.BlockSpec((16, RO...]
where the time goes in v2:
time: 92.2 us; the launch traced here: 91.9 us
  Pallas kernels  91.9 us (100%)
    pallas_call x1, Pallas kernels, main_stage(): pl.pallas_call(main_kernel, in_specs=[pl.BlockSpec(memory_space=pltpu.SME...  86 us
    pallas_call x1, Pallas kernels, last_stage(): pl.pallas_call(last_kernel, grid=(STEPS,), in_specs=[pl.BlockSpec((16, RO...  5.88 us

profile of v2, /device:TPU:1, one launch (start us, length us, event | category | flops | bytes accessed | tf_op | source)
XLA Modules:
  0.0 91.9 jit_solution(3908358435149881444)
XLA Ops:
  0.0 86.0 %main.1.z_ref = f32[16,128,256]{2,1,0:T(8,128)} custom-call(f32[4,4]{1,0:T(4,128)} %wgt_ref.1, f32[128,4096]{1,0:T(8,128)} %bitcast.3, f32[128,4096]{1,0:T(8,128)} %bitcast.4, f32[32,2,8,128]{3,2,1,0:T(8,128)} %constant.14.clone.tw_any, bf16[2,2,256,256]{3,2,1,0:T(8,128)(2,1)} %constant.10.clone.wr_any, bf16[2,256,256]{2,1,0:T(8,128)(2,1)} %constant.11.clone.wf_any, ...), custom_call_target="tpu_custom_call" | custom-call | tf_op jit(solution)/shard_map/main/pallas_call | solution.py:478
  86.0 5.9 %last.1 = f32[128,4096]{1,0:T(8,128)} custom-call(f32[16,128,256]{2,1,0:T(8,128)} %main.1.z_ref), custom_call_target="tpu_custom_call" | custom-call | tf_op jit(solution)/shard_map/last/pallas_call | solution.py:527

commit v3 on v2

--- a/solution.py
+++ b/solution.py
@@ -157,7 +157,7 @@
     return hi, lo
 
 
-ROWS = 16
+ROWS = 64
 STEPS = 128 // ROWS
 GROUP = 4
 FLAT = pl.DeviceIdType.LOGICAL

time: 92.2 us -> 89.1 us (0.966)
  Pallas kernels: 91.9 us -> 88.9 us
    pallas_call x1, Pallas kernels: 5.88 us -> 2.85 us  [last_stage(): pl.pallas_call(last_kernel, grid=(STEPS,), in_specs=[pl.BlockSpec((16, RO...]
where the time goes in v3:
time: 89.1 us; the launch traced here: 88.9 us
  Pallas kernels  88.9 us (100%)
    pallas_call x1, Pallas kernels, main_stage(): pl.pallas_call(main_kernel, in_specs=[pl.BlockSpec(memory_space=pltpu.SME...  86 us
    pallas_call x1, Pallas kernels, last_stage(): pl.pallas_call(last_kernel, grid=(STEPS,), in_specs=[pl.BlockSpec((16, RO...  2.85 us

profile of v3, /device:TPU:1, one launch (start us, length us, event | category | flops | bytes accessed | tf_op | source)
XLA Modules:
  0.0 88.9 jit_solution(10428460089595741432)
XLA Ops:
  0.0 86.0 %main.1.z_ref = f32[16,128,256]{2,1,0:T(8,128)} custom-call(f32[4,4]{1,0:T(4,128)} %wgt_ref.1, f32[128,4096]{1,0:T(8,128)} %bitcast.3, f32[128,4096]{1,0:T(8,128)} %bitcast.4, f32[32,2,8,128]{3,2,1,0:T(8,128)} %constant.14.clone.tw_any, bf16[2,2,256,256]{3,2,1,0:T(8,128)(2,1)} %constant.10.clone.wr_any, bf16[2,256,256]{2,1,0:T(8,128)(2,1)} %constant.11.clone.wf_any, ...), custom_call_target="tpu_custom_call" | custom-call | tf_op jit(solution)/shard_map/main/pallas_call | solution.py:478
  86.0 2.8 %last.1 = f32[128,4096]{1,0:T(8,128)} custom-call(f32[16,128,256]{2,1,0:T(8,128)} %main.1.z_ref), custom_call_target="tpu_custom_call" | custom-call | tf_op jit(solution)/shard_map/last/pallas_call | solution.py:527

commit v4 on v3

--- a/solution.py
+++ b/solution.py
@@ -49,7 +49,12 @@
         row=np.stack([hi_lo(first), hi_lo(fwd)]),
         colf=hi_lo(fwd.T),
         coli=hi_lo(fwd),
-        back=np.stack([hi_lo(last), hi_lo(fwd)]),
+        back=np.stack(
+            [
+                np.stack([hi_lo(m.reshape(2, 2, 64, 256)[:, h].reshape(128, 256)) for h in range(2)])
+                for m in (last, fwd)
+            ]
+        ),
         twid=twid,
     )
 
@@ -159,7 +164,7 @@
 
 ROWS = 64
 STEPS = 128 // ROWS
-GROUP = 4
+GROUP = 8
 FLAT = pl.DeviceIdType.LOGICAL
 
 
@@ -277,12 +282,16 @@
         ret_ref[half, A * j + t, 1] = m
 
 
-def back_matmul(k, in_ref, tw_ref, w_ref, z_ref):
-    parts = [in_ref[h, 8 * k + d, c] for c in range(2) for h in range(2) for d in range(8)]
+def back_matmul(half, k, in_ref, w_ref):
+    parts = [in_ref[half, 8 * k + d, c] for c in range(2) for d in range(8)]
     hi, lo = split(jnp.concatenate(parts, axis=0).T)
     sel = jnp.minimum(k, 1)
     dot = functools.partial(jnp.dot, preferred_element_type=F32)
-    Z = dot(hi, w_ref[sel, 0]) + (dot(lo, w_ref[sel, 0]) + dot(hi, w_ref[sel, 1]))
+    whi, wlo = w_ref[sel, half, 0], w_ref[sel, half, 1]
+    return dot(hi, whi) + (dot(lo, whi) + dot(hi, wlo))
+
+
+def back_twiddle(k, Z, tw_ref, z_ref):
     c, s = tw_ref[k, 0, 0:1], tw_ref[k, 1, 0:1]
     r, m = Z[:, 0:L], Z[:, L : 2 * L]
     z_ref[k, :, 0:L] = r * c - m * s
@@ -297,7 +306,29 @@
 ):
     mybin, mytile = lax.axis_index("bin"), lax.axis_index("tile")
     me = mybin * 32 + mytile
-    mygroup, mypart = mybin * 4 + lax.div(mytile, 8), lax.rem(mytile, 8)
+    myz, myx = lax.div(mytile, 8), lax.rem(lax.div(mytile, 2), 4)
+    myy = 2 * lax.rem(mytile, 2) + lax.div(mybin, 2)
+    mycore = lax.rem(mybin, 2)
+    mygroup = 8 * lax.rem(myz, 2) + 4 * lax.rem(myx, 2) + mybin
+    mysid = 8 * mygroup + 4 * lax.div(myz, 2) + 2 * lax.div(myx, 2) + lax.rem(mytile, 2)
+
+    def group_at(i):
+        og = jnp.where(lax.rem(i, 2) == 0, 15 - lax.div(i, 2), lax.div(i, 2))
+        zb = myz + lax.div(og, 8)
+        xb = myx + lax.rem(lax.div(og, 4), 2)
+        yb = myy + lax.rem(lax.div(og, 2), 2)
+        core = lax.rem(mycore + og, 2)
+        k = 8 * lax.rem(zb, 2) + 4 * lax.rem(xb, 2) + 2 * lax.rem(yb, 2) + core
+        z = [lax.rem(zb + 2 * p, 4) for p in range(2)]
+        x = [lax.rem(xb + 2 * p, 4) for p in range(2)]
+        y = [lax.rem(yb + 2 * p, 4) for p in range(2)]
+        base = 32 * core + 64 * lax.rem(yb, 2)
+        targets = []
+        for p in (0, 7, 1, 6, 2, 5, 4, 3):
+            pz, px, py = z[p // 4], x[p // 2 % 2], y[p % 2]
+            sid = 8 * k + 4 * lax.div(pz, 2) + 2 * lax.div(px, 2) + lax.div(py, 2)
+            targets.append((sid, base + 8 * pz + 2 * px + lax.div(py, 2)))
+        return og, k, targets
 
     barrier = pltpu.get_barrier_semaphore()
 
@@ -331,8 +362,8 @@
     lax.fori_loop(1, DEV, greet, 0)
     tabs[0].wait()
 
-    def go(half, dest, comp):
-        at = (half, dest) if comp is None else (half, dest, comp)
+    def go(half, sid, dest, comp):
+        at = (half, sid) if comp is None else (half, sid, comp)
         to = (half, me) if comp is None else (half, me, comp)
         pltpu.make_async_remote_copy(
             src_ref=send_ref.at[at],
@@ -354,15 +385,15 @@
             return lax.fori_loop(0, 4, step, carry)
 
         def matmul_step(i, carry):
-            k = lax.rem(mygroup + i, 16)
+            og, k, targets = group_at(i)
             row_matmul(comp, k, wr_ref, yr_ref, send_ref)
 
-            @pl.when(i > 0)
+            @pl.when(og > 0)
             def _():
-                go(0, 8 * k + mypart, comp)
-
-            for e in range(1, 8):
-                go(0, 8 * k + lax.rem(mypart + e, 8), comp)
+                go(0, *targets[0], comp)
+
+            for sid, dest in targets[1:]:
+                go(0, sid, dest, comp)
             return carry
 
         lax.fori_loop(0, 4, some_rows, 0)
@@ -375,14 +406,21 @@
     rows_of(1)
     for half in range(2):
         pltpu.make_async_copy(
-            send_ref.at[half, me], recv_ref.at[half, me], go_recv.at[half]
+            send_ref.at[half, mysid], recv_ref.at[half, me], go_recv.at[half]
         ).start()
 
     def second(i, carry):
-        go(1, 8 * lax.rem(mygroup + lax.div(i, 8), 16) + lax.rem(mypart + i, 8), None)
+        og, _, targets = group_at(i)
+
+        @pl.when(og > 0)
+        def _():
+            go(1, *targets[0], None)
+
+        for sid, dest in targets[1:]:
+            go(1, sid, dest, None)
         return carry
 
-    lax.fori_loop(1, DEV, second, 0)
+    lax.fori_loop(0, 16, second, 0)
     for t in tabs[2:]:
         t.wait()
 
@@ -391,7 +429,7 @@
     w = [[wgt_ref[j, b] * scale for b in range(j + 1)] for j in range(BINS)]
 
     def half_step(half, carry):
-        packed = jnp.logical_and(sub == 0, jnp.logical_and(me == 0, half == 0))
+        packed = jnp.logical_and(sub == 0, jnp.logical_and(mysid == 0, half == 0))
         pltpu.make_async_copy(send_ref.at[half], recv_ref.at[half], go_recv.at[half]).wait()
 
         def forward(b, c):
@@ -399,7 +437,7 @@
             return c
 
         def middle(g, c):
-            col_middle(half, g, me, packed, w, tw_ref, wf_ref, wi_ref, y_ref, z_ref)
+            col_middle(half, g, mysid, packed, w, tw_ref, wf_ref, wi_ref, y_ref, z_ref)
             return c
 
         def inverse(i, c):
@@ -409,29 +447,34 @@
             def ret(dest):
                 pltpu.make_async_remote_copy(
                     src_ref=ret_ref.at[half, dest],
-                    dst_ref=land_ref.at[half, me],
+                    dst_ref=land_ref.at[half, mysid],
                     send_sem=ret_send.at[half],
                     recv_sem=ret_recv.at[half, mygroup],
                     device_id=dest,
                     device_id_type=FLAT,
                 ).start()
 
-            def ret_step(e, c2):
-                z = lax.rem(lax.div(mytile, 8) + lax.div(e, 8), 4)
-                ret(32 * j + 8 * z + lax.rem(mypart + e, 8))
+            def ret_step(q, c2):
+                zb, xb = myz + lax.div(q, 2), myx + lax.rem(q, 2)
+                z = [lax.rem(zb + 2 * p, 4) for p in range(2)]
+                x = [lax.rem(xb + 2 * p, 4) for p in range(2)]
+                h = [lax.rem(mytile + p, 2) for p in range(2)]
+
+                @pl.when(i + q > 0)
+                def _():
+                    ret(32 * j + 8 * z[0] + 2 * x[0] + h[0])
+
+                for p in (7, 1, 6, 2, 5, 4, 3):
+                    ret(32 * j + 8 * z[p // 4] + 2 * x[p // 2 % 2] + h[p % 2])
                 return c2
 
-            @pl.when(i > 0)
-            def _():
-                ret(32 * j + mytile)
-
-            return lax.fori_loop(1, 32, ret_step, c)
+            return lax.fori_loop(0, 4, ret_step, c)
 
         lax.fori_loop(0, BINS, forward, 0)
         lax.fori_loop(0, A // GROUP, middle, 0)
         lax.fori_loop(0, BINS, inverse, 0)
         pltpu.make_async_copy(
-            ret_ref.at[half, me], land_ref.at[half, me], ret_recv.at[half, mygroup]
+            ret_ref.at[half, me], land_ref.at[half, mysid], ret_recv.at[half, mygroup]
         ).start()
         return carry
 
@@ -440,20 +483,27 @@
     def write(k):
         return pltpu.make_async_copy(last_ref.at[k], out_ref.at[k], out_sem.at[k])
 
-    def back_step(i, carry):
-        b = lax.rem(mybin + 4 - lax.div(i, 4), 4)
-        z = lax.rem(lax.div(mytile, 8) + 4 - lax.rem(i, 4), 4)
-        k = 4 * b + z
-        eight = pl.ds(pl.multiple_of(8 * k, 8), 8)
-        for half in range(2):
+    def back_of(half):
+        def back_step(i, carry):
+            b = lax.rem(mybin + 4 - lax.div(i, 4), 4)
+            q = lax.rem(i, 4)
+            k = 8 * lax.rem(myz + lax.div(q, 2), 2) + 4 * lax.rem(myx + q, 2) + b
+            eight = pl.ds(pl.multiple_of(8 * k, 8), 8)
             pltpu.make_async_copy(
                 ret_ref.at[half, eight], land_ref.at[half, eight], ret_recv.at[half, k]
             ).wait()
-        back_matmul(k, land_ref, tw_ref, wb_ref, last_ref)
-        write(k).start()
-        return carry
-
-    lax.fori_loop(0, 16, back_step, 0)
+            Z = back_matmul(half, k, land_ref, wb_ref)
+            if half == 0:
+                last_ref[k] = Z
+            else:
+                back_twiddle(k, last_ref[k] + Z, tw_ref, last_ref)
+                write(k).start()
+            return carry
+
+        lax.fori_loop(0, 16, back_step, 0)
+
+    back_of(0)
+    back_of(1)
 
     def finish(half, carry):
         for src, sem in ((send_ref, go_send), (ret_ref, ret_send)):
@@ -485,7 +535,7 @@
             pltpu.VMEM((2, 2, 256, 256), BF16),
             pltpu.VMEM((2, 256, 256), BF16),
             pltpu.VMEM((2, 256, 256), BF16),
-            pltpu.VMEM((2, 2, 256, 256), BF16),
+            pltpu.VMEM((2, 2, 2, 128, 256), BF16),
             pltpu.VMEM((2, 128, N), F32),
             pltpu.VMEM((16, 128, 256), F32),
             pltpu.VMEM((2, DEV, 2, 2, 8, L), F32),

time: 89.1 us -> 87.9 us (0.987)
  Pallas kernels: 88.9 us -> 87.6 us
    pallas_call x1, Pallas kernels: 86 us -> 84.8 us  [main_stage(): pl.pallas_call(main_kernel, in_specs=[pl.BlockSpec(memory_space=pltpu.SME...]
where the time goes in v4:
time: 87.9 us; the launch traced here: 87.7 us
  Pallas kernels  87.6 us (100%)
    pallas_call x1, Pallas kernels, main_stage(): pl.pallas_call(main_kernel, in_specs=[pl.BlockSpec(memory_space=pltpu.SME...  84.8 us
    pallas_call x1, Pallas kernels, last_stage(): pl.pallas_call(last_kernel, grid=(STEPS,), in_specs=[pl.BlockSpec((16, RO...  2.85 us

profile of v4, /device:TPU:1, one launch (start us, length us, event | category | flops | bytes accessed | tf_op | source)
XLA Modules:
  0.0 87.7 jit_solution(6520515696284631763)
XLA Ops:
  0.0 84.8 %main.1.z_ref = f32[16,128,256]{2,1,0:T(8,128)} custom-call(f32[4,4]{1,0:T(4,128)} %wgt_ref.1, f32[128,4096]{1,0:T(8,128)} %bitcast.3, f32[128,4096]{1,0:T(8,128)} %bitcast.4, f32[32,2,8,128]{3,2,1,0:T(8,128)} %constant.14.clone.tw_any, bf16[2,2,256,256]{3,2,1,0:T(8,128)(2,1)} %constant.10.clone.wr_any, bf16[2,256,256]{2,1,0:T(8,128)(2,1)} %constant.11.clone.wf_any, ...), custom_call_target="tpu_custom_call" | custom-call | tf_op jit(solution)/shard_map/main/pallas_call | solution.py:528
  84.8 2.8 %last.1 = f32[128,4096]{1,0:T(8,128)} custom-call(f32[16,128,256]{2,1,0:T(8,128)} %main.1.z_ref), custom_call_target="tpu_custom_call" | custom-call | tf_op jit(solution)/shard_map/last/pallas_call | solution.py:577

commit v5 on v4

--- a/solution.py
+++ b/solution.py
@@ -332,10 +332,20 @@
 
     barrier = pltpu.get_barrier_semaphore()
 
-    def greet(i, carry):
-        pl.semaphore_signal(
-            barrier, inc=1, device_id=lax.rem(me + i, DEV), device_id_type=FLAT
-        )
+    def greet(q, carry):
+        core, h = lax.rem(mybin + q, 2), lax.div(mybin, 2)
+        xs = [2 * lax.rem(myx + o, 4) for o in (2, 1, 3, 0)]
+        y = lax.rem(myy + 2 + lax.div(q, 2), 4)
+        base = 64 * lax.rem(y, 2) + 32 * core + lax.div(y, 2)
+        for oz in (2, 1, 3, 0):
+            z = 8 * lax.rem(myz + oz, 4)
+            for x in xs:
+                dest = base + z + x
+
+                @pl.when(dest != me)
+                def _():
+                    pl.semaphore_signal(barrier, inc=1, device_id=dest, device_id_type=FLAT)
+
         return carry
 
     tabs = [
@@ -359,7 +369,7 @@
         load(1, i).start()
     for t in tabs[2:]:
         t.start()
-    lax.fori_loop(1, DEV, greet, 0)
+    lax.fori_loop(0, 8, greet, 0)
     tabs[0].wait()
 
     def go(half, sid, dest, comp):

time: 87.9 us -> 87.7 us (level)
  no operation moved by 1% of the time
where the time goes in v5:
time: 87.7 us; the launch traced here: 87.5 us
  Pallas kernels  87.5 us (100%)
    pallas_call x1, Pallas kernels, main_stage(): pl.pallas_call(main_kernel, in_specs=[pl.BlockSpec(memory_space=pltpu.SME...  84.7 us
    pallas_call x1, Pallas kernels, last_stage(): pl.pallas_call(last_kernel, grid=(STEPS,), in_specs=[pl.BlockSpec((16, RO...  2.85 us

profile of v5, /device:TPU:1, one launch (start us, length us, event | category | flops | bytes accessed | tf_op | source)
XLA Modules:
  0.0 87.5 jit_solution(17364688951290367633)
XLA Ops:
  0.0 84.7 %main.1.z_ref = f32[16,128,256]{2,1,0:T(8,128)} custom-call(f32[4,4]{1,0:T(4,128)} %wgt_ref.1, f32[128,4096]{1,0:T(8,128)} %bitcast.3, f32[128,4096]{1,0:T(8,128)} %bitcast.4, f32[32,2,8,128]{3,2,1,0:T(8,128)} %constant.14.clone.tw_any, bf16[2,2,256,256]{3,2,1,0:T(8,128)(2,1)} %constant.10.clone.wr_any, bf16[2,256,256]{2,1,0:T(8,128)(2,1)} %constant.11.clone.wf_any, ...), custom_call_target="tpu_custom_call" | custom-call | tf_op jit(solution)/shard_map/main/pallas_call | solution.py:538
  84.7 2.8 %last.1 = f32[128,4096]{1,0:T(8,128)} custom-call(f32[16,128,256]{2,1,0:T(8,128)} %main.1.z_ref), custom_call_target="tpu_custom_call" | custom-call | tf_op jit(solution)/shard_map/last/pallas_call | solution.py:587
